TPU v7x, 512 devices: a whole 4x4x16 slice. The times are simulated.
512 devices in a mesh: section: 2 (over x_hi), dp: 8 (over y, core), tensor: 32 (over x_lo, z).
Axes of the slice: x: 4 (x_hi: 2, x_lo: 2; x = x_hi * 2 + x_lo), y: 4, z: 16, core: 2. Of those that a mesh axis runs over, the one named last changes fastest.
Arguments:
- tokens_in: bfloat16 [2, 7168, 2048], P(None, 'tensor', 'dp'), may hold values from -47 to 47
- section_proj: bfloat16 [2, 7168, 7168], P('section', 'tensor'), may hold values from -0.0625 to 0.0625
- section_gain: bfloat16 [2, 7168], P('section', 'tensor'), may hold values from 0.099609375 to 1.8984375
- final_gain: bfloat16 [7168], P('tensor'), may hold values from 0.099609375 to 1.8984375
- score_weight: bfloat16 [7168], P('tensor'), may hold values from -0.0625 to 0.0625
- labels: int32 [2, 2048], P(None, 'dp'), may hold values from 0 to 2
- loss_mask: int32 [2, 2048], P(None, 'dp'), may hold values 0 or 1
- segment_ids: int32 [2, 2048], P(None, 'dp'), may hold values from 0 to 15, never falling along the last dimension, each value on 1 to 512 neighbouring positions
Outputs:
- section_out: bfloat16 [2, 2, 7168, 2048], P('section', None, 'tensor', 'dp')
- segment_loss: float32 [2, 16], replicated
Inputs may be any that keep to these rules, and one draw needn't show every extreme that they name: `segment_ids`: within a micro-batch segment numbers never fall along the tokens; each segment has 1 to 512 tokens.
All inputs are finite; a program needn't handle non-finite values. No bound on the sum of `loss_mask` on one device may be relied on, other than what follows from the above.
Results may differ from a plain program's by a relative error of at most 0.0045.
Values may be sent and summed in bfloat16 or wider, within the bound.
No kernel may reach another device: no remote copies, remote signals or barrier semaphores. Data moves between devices by JAX's collectives and lax.ppermute only.
A program may use at most 64 MiB of HBM per device.

v0:
```python
import jax
import jax.numpy as jnp
from jax import lax
from jax.sharding import PartitionSpec as P

D = 7168
SEGS = 16
epsilon = 1e-05


def passed_along(shard, axis, by):
    count = lax.axis_size(axis)
    pairs = [(i, i + by) for i in range(count) if 0 <= i + by < count]
    return lax.ppermute(shard, axis, pairs)


def body(
    tokens_in, section_proj, section_gain, final_gain, score_weight, labels, loss_mask, segment_ids
):
    section_index = lax.axis_index("section")
    weight_local = section_proj[0]
    gain_local = section_gain[0]
    head_vector = final_gain.astype(jnp.float32) * score_weight.astype(jnp.float32)
    micro_count = tokens_in.shape[0]
    received = jnp.zeros_like(tokens_in[0])
    produced = []
    score_list = []
    for moment in range(micro_count + 1):
        if moment < micro_count:
            fresh_rows = tokens_in[moment]
        else:
            fresh_rows = jnp.zeros_like(tokens_in[0])
        incoming = jnp.where(section_index == 0, fresh_rows, received)
        apply_as_float = incoming.astype(jnp.float32)
        apply_squares = lax.psum(jnp.sum(apply_as_float * apply_as_float, axis=0), "tensor")
        apply_inv_root = lax.rsqrt(apply_squares / D + epsilon)[None, :]
        normed = (apply_as_float * apply_inv_root * gain_local.astype(jnp.float32)[:, None]).astype(
            jnp.bfloat16
        )
        mixed = jnp.dot(
            weight_local,
            lax.all_gather(normed, "tensor", axis=0, tiled=True),
            preferred_element_type=jnp.float32,
        )
        result_rows = (apply_as_float + jax.nn.silu(mixed)).astype(jnp.bfloat16)
        produced.append(result_rows)
        if moment < micro_count:
            received = passed_along(result_rows, "section", 1)
        if moment >= 1:
            as_float = result_rows.astype(jnp.float32)
            squares_part = jnp.sum(as_float * as_float, axis=0)
            squares = lax.psum(squares_part, "tensor")
            inv_root = lax.rsqrt(squares / D + epsilon)
            partial_score = jnp.sum(as_float * inv_root[None, :] * head_vector[:, None], axis=0)
            score_list.append(lax.psum(partial_score, "tensor"))
    section_out = jnp.where(
        section_index == 0, jnp.stack(produced[:micro_count]), jnp.stack(produced[1:])
    )[None]
    segment_range = lax.broadcasted_iota(jnp.int32, (1, SEGS), 1)
    sum_rows = []
    count_rows = []
    for micro in range(micro_count):
        target = labels[micro].astype(jnp.float32) - 1.0
        weight_mask = loss_mask[micro].astype(jnp.float32)
        offset_err = score_list[micro] - target
        squared = weight_mask * offset_err * offset_err
        member = (segment_ids[micro][:, None] == segment_range).astype(jnp.float32)
        sum_rows.append(jnp.dot(squared, member, precision=lax.Precision.HIGHEST))
        count_rows.append(jnp.dot(weight_mask, member, precision=lax.Precision.HIGHEST))
    live_section = (section_index == 1).astype(jnp.float32)
    loss_sums, counted = lax.psum(
        (jnp.stack(sum_rows) * live_section, jnp.stack(count_rows) * live_section),
        ("section", "dp"),
    )
    segment_loss = loss_sums / jnp.maximum(counted, 1.0)
    return (section_out, segment_loss)


def solution(mesh):
    in_specs = (
        P(None, "tensor", "dp"),
        P("section", "tensor", None),
        P("section", "tensor"),
        P("tensor"),
        P("tensor"),
        P(None, "dp"),
        P(None, "dp"),
        P(None, "dp"),
    )
    out_specs = (P("section", None, "tensor", "dp"), P())
    return jax.shard_map(body, mesh=mesh, in_specs=in_specs, out_specs=out_specs, check_vma=False)
```

profile of v0, /device:TPU:1, one launch (start us, length us, event | category | flops | bytes accessed | tf_op | source)
XLA Modules:
  0.0 791.1 jit_solution(1438535462206001825)
XLA Ops:
  7.2 0.0 copy-start
  7.2 0.0 all-gather.4.cloned.1.call-start
  7.2 1.1 fusion.29
  8.3 57.2 %psum.63 = f32[256]{0:T(256)S(1)} all-reduce(f32[256]{0:T(256)S(1)} %fusion.29), channel_id=1, replica_groups=mesh['section'=2,'dp'=8,'tensor'=32] {'tensor'}, use_global_device_ids=true, to_apply=%region_1.2 | all-reduce | flops 256 | bytes 2048 | tf_op jit(solution)/shard_map/psum | solution.py:35
  65.5 0.7 convert_element_type.103
  66.2 0.0 copy-start.3
  66.2 0.5 copy-done.3
  66.8 1.6 fusion.31
  68.4 0.0 all-gather.4.cloned.1.call-update
  68.4 0.0 copy-start.1
  68.5 0.0 all-gather.6.cloned.1.call-start
  68.5 124.1 %all-gather.4.cloned.1.call-done = bf16[7168,256]{1,0:T(8,128)(2,1)} async-done(((bf16[224,256]{1,0:T(8,128)(2,1)}), bf16[7168,256]{1,0:T(8,128)(2,1)}) %all-gather.4.cloned.1.call-update) | async-done | bytes 3670032 | tf_op jit(solution)/shard_map/all_gather | solution.py:42
  192.6 0.0 copy-done
  192.6 3.1 fusion.32
  195.7 0.0 copy-start.2
  195.7 3.6 collective-permute-start
  199.3 2.0 collective-permute-done
  201.3 0.0 copy-done.1
  201.3 0.6 fusion.21
  201.9 0.0 copy-done.2
  201.9 49.3 %psum.64 = f32[256]{0:T(256)S(1)} all-reduce(f32[256]{0:T(256)} %get-tuple-element.10), channel_id=1, replica_groups=mesh['section'=2,'dp'=8,'tensor'=32] {'tensor'}, use_global_device_ids=true, to_apply=%region_3.4 | all-reduce | flops 256 | bytes 2048 | tf_op jit(solution)/shard_map/psum | solution.py:35
  251.2 1.4 fusion.23
  252.6 0.0 all-gather.6.cloned.1.call-update
  252.6 0.0 all-gather.8.cloned.1.call-start
  252.7 144.1 %all-gather.6.cloned.1.call-done = bf16[7168,256]{1,0:T(8,128)(2,1)} async-done(((bf16[224,256]{1,0:T(8,128)(2,1)}), bf16[7168,256]{1,0:T(8,128)(2,1)}) %all-gather.6.cloned.1.call-update) | async-done | bytes 3670032 | tf_op jit(solution)/shard_map/all_gather | solution.py:42
  396.8 3.6 fusion.15
  400.5 3.6 collective-permute-start.1
  404.1 2.0 collective-permute-done.1
  406.1 0.1 fusion.25
  406.1 49.3 %psum.65 = f32[256]{0:T(256)S(1)} all-reduce(f32[256]{0:T(256)S(1)} %fusion.25), channel_id=1, replica_groups=mesh['section'=2,'dp'=8,'tensor'=32] {'tensor'}, use_global_device_ids=true, to_apply=%region_5.6 | all-reduce | flops 256 | bytes 2048 | tf_op jit(solution)/shard_map/psum | solution.py:35
  455.4 1.4 fusion.27
  456.8 0.0 all-gather.8.cloned.1.call-update
  456.8 0.8 fusion.49
  457.6 0.0 copy-start.4
  457.6 0.0 copy-start.5
  457.6 0.5 copy-done.4
  458.1 0.9 fusion.39
  459.0 0.0 copy-done.5
  459.0 0.9 fusion.41
  460.0 0.6 maximum_multiply_fusion.1
  460.5 1.2 convert_multiply_fusion.10
  461.7 1.4 slice_convert_fusion.1
  463.1 1.4 convert_add_fusion.4
  464.5 136.4 %all-gather.8.cloned.1.call-done = bf16[7168,256]{1,0:T(8,128)(2,1)} async-done(((bf16[224,256]{1,0:T(8,128)(2,1)}), bf16[7168,256]{1,0:T(8,128)(2,1)}) %all-gather.8.cloned.1.call-update) | async-done | bytes 3670032 | tf_op jit(solution)/shard_map/all_gather | solution.py:42
  600.9 3.6 fusion.18
  604.5 48.4 %all-reduce.1 = (f32[256]{0:T(256)S(1)}, f32[256]{0:T(256)S(1)}) all-reduce(f32[256]{0:T(256)} %get-tuple-element.18, f32[256]{0:T(256)} %get-tuple-element.20), channel_id=1, replica_groups=mesh['section'=2,'dp'=8,'tensor'=32] {'tensor'}, use_global_device_ids=true, to_apply=%region_7.8 | all-reduce | flops 512 | bytes 4096 | tf_op jit(solution)/shard_map/psum | solution.py:52
  653.0 0.7 fusion.17
  653.7 46.4 %all-reduce = (f32[256]{0:T(256)S(1)}, f32[256]{0:T(256)S(1)}) all-reduce(f32[256]{0:T(256)S(1)} %get-tuple-element.3, f32[256]{0:T(256)S(1)} %get-tuple-element.2), channel_id=1, replica_groups=mesh['section'=2,'dp'=8,'tensor'=32] {'tensor'}, use_global_device_ids=true, to_apply=%region_13.14 | all-reduce | flops 512 | bytes 4096 | tf_op jit(solution)/shard_map/psum | solution.py:55
  700.1 0.7 multiply_multiply_fusion.1
  700.8 0.9 fusion.42
  701.6 0.7 multiply_multiply_fusion
  702.3 0.8 fusion.40
  703.2 79.2 %all-reduce.2 = (f32[2,16]{1,0:T(2,128)S(1)}, f32[2,16]{1,0:T(2,128)S(1)}) all-reduce(f32[2,16]{1,0:T(2,128)S(1)} %maximum_multiply_fusion, f32[2,16]{1,0:T(2,128)} %maximum_multiply_fusion.1), channel_id=1, replica_groups=mesh['section'=2,'dp'=8,'tensor'=32] {'section','dp'}, use_global_device_ids=true, to_apply=%region_14.15 | all-reduce | flops 64 | bytes 512 | tf_op jit(solution)/shard_map/psum | solution.py:71
  782.4 0.6 maximum_divide_fusion
  782.9 1.6 maximum_select_fusion
  (5 shorter events, 0.1 us)
Async XLA Ops:
  7.2 185.4 %copy-start = (bf16[1,224,7168]{2,1,0:T(8,128)(2,1)S(1)}, bf16[1,224,7168]{2,1,0:T(8,128)(2,1)}, u32[]{:S(2)}) copy-start(bf16[1,224,7168]{2,1,0:T(8,128)(2,1)} %param.9) | copy-start | bytes 9633796
  7.2 185.4 %all-gather.4.cloned.1.call-start = ((), (), s32[]{:S(2)}) async-start(), calls=%async_computation | async-start | bytes 3784704 | tf_op jit(solution)/shard_map/all_gather | solution.py:42
  66.2 0.5 copy-start.3
  68.4 132.9 %copy-start.1 = (bf16[2,224,256]{2,1,0:T(8,128)(2,1)S(1)}, bf16[2,224,256]{2,1,0:T(8,128)(2,1)}, u32[]{:S(2)}) copy-start(bf16[2,224,256]{2,1,0:T(8,128)(2,1)} %param.8) | copy-start | bytes 688132
  68.5 328.4 %all-gather.6.cloned.1.call-start = ((), (), s32[]{:S(2)}) async-start(), calls=%async_computation.1 | async-start | bytes 3784704 | tf_op jit(solution)/shard_map/all_gather | solution.py:42
  195.7 6.3 copy-start.2
  195.7 5.6 collective-permute-start
  252.6 348.3 %all-gather.8.cloned.1.call-start = ((), (), s32[]{:S(2)}) async-start(), calls=%async_computation.2 | async-start | bytes 3784704 | tf_op jit(solution)/shard_map/all_gather | solution.py:42
  400.5 5.6 collective-permute-start.1
  457.6 0.5 copy-start.4
  457.6 1.4 copy-start.5
Sparse Core Ops, SparseCore 0:
  68.6 123.9 all-gather.3
  252.7 144.0 all-gather.5
  456.9 143.8 all-gather.7
where the time goes:
time: 792 us; the launch traced here: 791 us
  waiting for transfers between devices  409 us (52%)
  blocking collectives  330 us (42%)
  other arithmetic  15.7 us (2%)
  matrix products  13.9 us (2%)
  between operations  13.8 us (2%)
    all_gather x3, waiting for transfers between devices, body(): lax.all_gather(normed, 'tensor', axis=0, tiled=True)  405 us
    psum x3, blocking collectives, body(): lax.psum(jnp.sum(apply_as_float * apply_as_float, axis=0), 'tensor')  156 us
    psum x1, blocking collectives, body(): lax.psum((jnp.stack(sum_rows) * live_section, jnp.stack(count_rows) * liv...  79.2 us
    psum x1, blocking collectives, body(): squares = lax.psum(squares_part, 'tensor')  48.4 us
    psum x1, blocking collectives, body(): score_list.append(lax.psum(partial_score, 'tensor'))  46.4 us
  transfers between devices with their start and end apart: 5, of which 5 were waited for; matrix products, arithmetic and copies ran while one was open for 1% of the time, Pallas kernels for 0%

commit v1 on v0

--- a/solution.py
+++ b/solution.py
@@ -39,7 +39,10 @@
         )
         mixed = jnp.dot(
             weight_local,
-            lax.all_gather(normed, "tensor", axis=0, tiled=True),
+            jnp.concatenate(
+                lax.all_to_all(jnp.stack([normed] * lax.axis_size("tensor")), "tensor", 0, 0),
+                axis=0,
+            ),
             preferred_element_type=jnp.float32,
         )
         result_rows = (apply_as_float + jax.nn.silu(mixed)).astype(jnp.bfloat16)

time: 792 us -> 808 us (1.020)
  blocking collectives: 330 us -> 683 us
  waiting for transfers between devices: 409 us -> 86.2 us
  between operations: 13.8 us -> 0.82 us
    all_gather x3 -> x0, waiting for transfers between devices: 405 us -> none  [body(): lax.all_gather(normed, 'tensor', axis=0, tiled=True)]
    all_to_all x0 -> x2, blocking collectives: none -> 280 us  [body(): lax.all_to_all(jnp.stack([normed] * lax.axis_size('tensor')), 'tensor', 0...]
    all_to_all x0 -> x1, waiting for transfers between devices: none -> 81.8 us  [body(): lax.all_to_all(jnp.stack([normed] * lax.axis_size('tensor')), 'tensor', 0...]
    psum x1, blocking collectives: 48.4 us -> 86.7 us  [body(): squares = lax.psum(squares_part, 'tensor')]
    psum x1, blocking collectives: 79.2 us -> 107 us  [body(): lax.psum((jnp.stack(sum_rows) * live_section, jnp.stack(count_rows) * liv...]
  transfers between devices with their start and end apart: 5 -> 3, of which waited for: 5 -> 3; matrix products, arithmetic and copies ran while one was open for 1% -> 0% of each run, Pallas kernels for 0% -> 0%
where the time goes in v1:
time: 808 us; the launch traced here: 807 us
  blocking collectives  683 us (85%)
  waiting for transfers between devices  86.2 us (11%)
  starting transfers between devices  14.7 us (2%)
  other arithmetic  10.6 us (1%)
  matrix products  8.57 us (1%)
    all_to_all x2, blocking collectives, body(): lax.all_to_all(jnp.stack([normed] * lax.axis_size('tensor')), 'tensor', 0...  280 us
    psum x3, blocking collectives, body(): lax.psum(jnp.sum(apply_as_float * apply_as_float, axis=0), 'tensor')  163 us
    psum x1, blocking collectives, body(): lax.psum((jnp.stack(sum_rows) * live_section, jnp.stack(count_rows) * liv...  107 us
    psum x1, blocking collectives, body(): squares = lax.psum(squares_part, 'tensor')  86.7 us
    all_to_all x1, waiting for transfers between devices, body(): lax.all_to_all(jnp.stack([normed] * lax.axis_size('tensor')), 'tensor', 0...  81.8 us
    psum x1, blocking collectives, body(): score_list.append(lax.psum(partial_score, 'tensor'))  46.3 us
  transfers between devices with their start and end apart: 3, of which 3 were waited for; matrix products, arithmetic and copies ran while one was open for 0% of the time, Pallas kernels for 0%

profile of v1, /device:TPU:1, one launch (start us, length us, event | category | flops | bytes accessed | tf_op | source)
XLA Modules:
  0.0 807.1 jit_solution(9101060022060152495)
XLA Ops:
  0.6 0.0 copy-start
  0.7 1.1 fusion.23
  1.8 57.2 %psum.63 = f32[256]{0:T(256)S(1)} all-reduce(f32[256]{0:T(256)S(1)} %fusion.23), channel_id=1, replica_groups=mesh['section'=2,'dp'=8,'tensor'=32] {'tensor'}, use_global_device_ids=true, to_apply=%region_1.2 | all-reduce | flops 256 | bytes 2048 | tf_op jit(solution)/shard_map/psum | solution.py:35
  59.0 0.7 convert_element_type.108
  59.7 0.0 copy-start.3
  59.7 1.0 fusion.45
  60.7 0.4 stack.31
  61.1 0.0 copy-start.1
  61.1 151.5 %all_to_all.15 = bf16[32,224,256]{2,1,0:T(8,128)(2,1)S(1)} all-to-all(bf16[32,224,256]{2,1,0:T(8,128)(2,1)S(1)} %stack.31), channel_id=1, replica_groups=mesh['section'=2,'dp'=8,'tensor'=32] {'tensor'}, dimensions={0} | all-to-all | bytes 7340032 | tf_op jit(solution)/shard_map/all_to_all | solution.py:43
  212.5 0.0 copy-done
  212.5 0.0 copy-done.1
  212.6 1.1 fusion.24
  213.6 0.0 copy-start.2
  213.6 4.4 collective-permute-start
  218.0 2.4 collective-permute-done
  220.4 0.1 fusion.27
  220.5 50.6 %psum.64 = f32[256]{0:T(256)S(1)} all-reduce(f32[256]{0:T(256)S(1)} %get-tuple-element.10), channel_id=1, replica_groups=mesh['section'=2,'dp'=8,'tensor'=32] {'tensor'}, use_global_device_ids=true, to_apply=%region_3.4 | all-reduce | flops 256 | bytes 2048 | tf_op jit(solution)/shard_map/psum | solution.py:35
  271.0 0.0 copy-done.2
  271.0 0.0 copy-done.3
  271.0 0.1 fusion.29
  271.1 0.4 stack.33
  271.6 128.8 %all_to_all.16 = bf16[32,224,256]{2,1,0:T(8,128)(2,1)S(1)} all-to-all(bf16[32,224,256]{2,1,0:T(8,128)(2,1)S(1)} %stack.33), channel_id=1, replica_groups=mesh['section'=2,'dp'=8,'tensor'=32] {'tensor'}, dimensions={0} | all-to-all | bytes 7340032 | tf_op jit(solution)/shard_map/all_to_all | solution.py:43
  400.4 1.7 fusion.17
  402.0 5.4 collective-permute-start.1
  407.4 2.1 collective-permute-done.1
  409.4 0.1 fusion.31
  409.5 55.4 %psum.65 = f32[256]{0:T(256)S(1)} all-reduce(f32[256]{0:T(256)S(1)} %fusion.31), channel_id=1, replica_groups=mesh['section'=2,'dp'=8,'tensor'=32] {'tensor'}, use_global_device_ids=true, to_apply=%region_5.6 | all-reduce | flops 256 | bytes 2048 | tf_op jit(solution)/shard_map/psum | solution.py:35
  464.9 0.8 fusion.33
  465.7 2.2 stack.36
  468.0 0.0 copy-start.4
  468.0 0.0 copy-start.5
  468.0 0.0 copy-start.9
  468.0 0.0 copy-start.10
  468.0 0.0 copy-start.6
  468.0 5.0 all-to-all-start.2
  473.0 0.0 copy-done.4
  473.0 0.0 copy-start.7
  473.0 0.0 copy-start.8
  473.0 0.0 copy-done.5
  473.0 0.2 fusion.41
  473.2 0.2 fusion.43
  473.5 0.6 maximum_multiply_fusion.1
  474.1 0.0 copy-done.9
  474.1 0.0 copy-done.10
  474.1 0.6 convert_multiply_fusion.9
  474.7 0.6 slice_convert_fusion.1
  475.3 0.0 copy-done.6
  475.3 0.6 convert_add_fusion.3
  475.9 81.8 %all-to-all-done.2 = bf16[32,224,256]{2,1,0:T(8,128)(2,1)} async-done(((bf16[32,224,256]{2,1,0:T(8,128)(2,1)}), bf16[32,224,256]{2,1,0:T(8,128)(2,1)}, u32[]{:S(2)}, u32[]{:S(2)}) %all-to-all-start.2) | async-done | bytes 3670048 | tf_op jit(solution)/shard_map/all_to_all | solution.py:43
  557.6 0.0 copy-done.7
  557.6 0.0 copy-done.8
  557.6 3.6 fusion.20
  561.3 86.7 %all-reduce.1 = (f32[256]{0:T(256)S(1)}, f32[256]{0:T(256)S(1)}) all-reduce(f32[256]{0:T(256)} %get-tuple-element.18, f32[256]{0:T(256)} %get-tuple-element.20), channel_id=1, replica_groups=mesh['section'=2,'dp'=8,'tensor'=32] {'tensor'}, use_global_device_ids=true, to_apply=%region_7.8 | all-reduce | flops 512 | bytes 4096 | tf_op jit(solution)/shard_map/psum | solution.py:55
  648.0 0.8 fusion.19
  648.8 46.3 %all-reduce = (f32[256]{0:T(256)S(1)}, f32[256]{0:T(256)S(1)}) all-reduce(f32[256]{0:T(256)S(1)} %get-tuple-element.3, f32[256]{0:T(256)S(1)} %get-tuple-element.2), channel_id=1, replica_groups=mesh['section'=2,'dp'=8,'tensor'=32] {'tensor'}, use_global_device_ids=true, to_apply=%region_13.14 | all-reduce | flops 512 | bytes 4096 | tf_op jit(solution)/shard_map/psum | solution.py:58
  695.1 0.7 multiply_multiply_fusion.1
  695.8 0.9 fusion.44
  696.7 0.7 multiply_multiply_fusion
  697.4 0.9 fusion.42
  698.3 106.7 %all-reduce.2 = (f32[2,16]{1,0:T(2,128)S(1)}, f32[2,16]{1,0:T(2,128)S(1)}) all-reduce(f32[2,16]{1,0:T(2,128)S(1)} %maximum_multiply_fusion, f32[2,16]{1,0:T(2,128)} %maximum_multiply_fusion.1), channel_id=1, replica_groups=mesh['section'=2,'dp'=8,'tensor'=32] {'section','dp'}, use_global_device_ids=true, to_apply=%region_14.15 | all-reduce | flops 64 | bytes 512 | tf_op jit(solution)/shard_map/psum | solution.py:74
  804.9 0.6 maximum_divide_fusion
  805.5 1.6 maximum_select_fusion
  (6 shorter events, 0.1 us)
Async XLA Ops:
  0.6 211.9 %copy-start = (bf16[1,224,7168]{2,1,0:T(8,128)(2,1)S(1)}, bf16[1,224,7168]{2,1,0:T(8,128)(2,1)}, u32[]{:S(2)}) copy-start(bf16[1,224,7168]{2,1,0:T(8,128)(2,1)} %param.9) | copy-start | bytes 9633796
  59.7 211.4 %copy-start.3 = (f32[1,224]{1,0:T(1,128)}, f32[1,224]{1,0:T(1,128)S(1)}, u32[]{:S(2)}) copy-start(f32[1,224]{1,0:T(1,128)S(1)} %convert_element_type.108) | copy-start | bytes 2692
  61.1 151.5 %copy-start.1 = (bf16[2,224,256]{2,1,0:T(8,128)(2,1)S(1)}, bf16[2,224,256]{2,1,0:T(8,128)(2,1)}, u32[]{:S(2)}) copy-start(bf16[2,224,256]{2,1,0:T(8,128)(2,1)} %param.8) | copy-start | bytes 688132
  213.6 57.4 %copy-start.2 = (bf16[224,256]{1,0:T(8,128)(2,1)}, bf16[224,256]{1,0:T(8,128)(2,1)S(1)}, u32[]{:S(2)}) copy-start(bf16[224,256]{1,0:T(8,128)(2,1)S(1)} %fusion.24) | copy-start | bytes 344068
  213.6 6.8 collective-permute-start
  402.0 7.4 collective-permute-start.1
  468.0 5.0 copy-start.4
  468.0 5.0 copy-start.5
  468.0 6.1 copy-start.9
  468.0 6.1 copy-start.10
  468.0 7.3 copy-start.6
  468.0 89.6 %all-to-all-start.2 = ((bf16[32,224,256]{2,1,0:T(8,128)(2,1)}), bf16[32,224,256]{2,1,0:T(8,128)(2,1)}, u32[]{:S(2)}, u32[]{:S(2)}) async-start(bf16[32,224,256]{2,1,0:T(8,128)(2,1)} %stack.36), calls=%async_computation.2 | async-start | bytes 7340032 | tf_op jit(solution)/shard_map/all_to_all | solution.py:43
  473.0 84.6 %copy-start.7 = (s32[1,256]{1,0:T(1,128)}, s32[1,256]{1,0:T(1,128)S(1)}, u32[]{:S(2)}) copy-start(s32[1,256]{1,0:T(1,128)S(1)} %get-tuple-element.13) | copy-start | bytes 3076
  473.0 84.6 %copy-start.8 = (s32[1,256]{1,0:T(1,128)}, s32[1,256]{1,0:T(1,128)S(1)}, u32[]{:S(2)}) copy-start(s32[1,256]{1,0:T(1,128)S(1)} %get-tuple-element.12) | copy-start | bytes 3076
